TPU v7x, 32 devices: a whole 2x2x4 slice. The times are simulated.
32 devices in a mesh: outer: 4 (over z), dev: 8 (over y, x, core).
Axes of the slice: x: 2, y: 2, z: 4, core: 2. Of those that a mesh axis runs over, the one named last changes fastest.
Arguments:
- partials: bfloat16 [32, 8192, 128], P(('outer', 'dev')), may hold values from -6 to 6
- p_old: bfloat16 [8192, 1024], P('dev'), may hold values from -0.0625 to 0.0625
- p_new: bfloat16 [8192, 1024], P('dev'), may hold values from -0.0625 to 0.0625
- weight: float32 [8192, 128], P('dev'), may hold values from -4 to 4
- m_old: float32 [1024, 128], P('dev'), may hold values from -96 to 96
- v_old: float32 [1024, 128], P('dev'), may hold values from 32 to 1280
Outputs:
- new_weight: float32 [8192, 128], P('dev')
- m_new: float32 [1024, 128], P('dev')
- v_new: float32 [1024, 128], P('dev')
All inputs are finite; a program needn't handle non-finite values.
Results may differ from a plain program's by a relative error of at most 0.0012.
Values may be sent and summed in bfloat16 or wider, within the bound.
A program may use at most 128 MiB of HBM per device.

v0:
```python
import jax
import jax.numpy as jnp
from jax import lax
from jax.sharding import PartitionSpec as P

beta_mean = 0.9
beta_square = 0.95
bias_mean = 0.9999734386011124
bias_square = 0.9940794707796659
adam_epsilon = 1e-08
step_scale = 0.5


def on_device(partials, p_old, p_new, weight, m_old, v_old):
    local_grad = partials[0].astype(jnp.float32)
    grad_rows = lax.psum_scatter(local_grad, "dev", scatter_dimension=0, tiled=True)
    basis = p_new.astype(jnp.float32)
    columns = basis
    projected = lax.psum_scatter(
        jnp.dot(columns.T, grad_rows, precision=lax.Precision.HIGHEST),
        "dev",
        scatter_dimension=0,
        tiled=True,
    )
    projected = lax.psum(projected, "outer")
    columns = p_new
    margin_rows = lax.psum_scatter(
        jnp.dot(columns.T, p_old, preferred_element_type=jnp.float32),
        "dev",
        scatter_dimension=0,
        tiled=True,
    )
    first_piece = lax.all_gather(m_old, "dev", axis=0, tiled=True)
    second_piece = lax.all_gather(v_old, "dev", axis=0, tiled=True)
    first = jnp.dot(margin_rows, first_piece, precision=lax.Precision.HIGHEST)
    second = jnp.dot(margin_rows * margin_rows, second_piece, precision=lax.Precision.HIGHEST)
    m_new = beta_mean * first + (1.0 - beta_mean) * projected
    v_new = beta_square * second + (1.0 - beta_square) * projected * projected
    direction = (m_new / bias_mean / (jnp.sqrt(v_new / bias_square) + adam_epsilon)).astype(
        jnp.bfloat16
    )
    columns = p_new
    update = jnp.dot(
        columns,
        lax.all_gather(direction, "dev", axis=0, tiled=True),
        preferred_element_type=jnp.float32,
    )
    new_weight = weight - step_scale * update
    return (new_weight, m_new, v_new)


def solution(mesh):
    in_specs = (
        P(("outer", "dev"), None, None),
        P("dev", None),
        P("dev", None),
        P("dev", None),
        P("dev", None),
        P("dev", None),
    )
    out_specs = (P("dev", None), P("dev", None), P("dev", None))
    return jax.shard_map(
        on_device, mesh=mesh, in_specs=in_specs, out_specs=out_specs, check_vma=False
    )
```

profile of v0, /device:TPU:0, one launch (start us, length us, event | category | flops | bytes accessed | tf_op | source)
XLA Modules:
  0.0 216.5 jit_solution(17691967801441322931)
XLA Ops:
  7.2 0.0 copy-start
  7.2 0.0 reduce-scatter.6.cloned.1.call-start
  7.2 3.9 %bitcast_convert_fusion = f32[8192,128]{1,0:T(8,128)} fusion(bf16[1,8192,128]{2,1,0:T(8,128)(2,1)} %param.6), kind=kLoop, calls=%fused_computation | loop fusion | flops 1048576 | bytes 6291456 | tf_op jit(solution)/shard_map/convert_element_type | solution.py:15
  11.2 0.0 reduce-scatter.6.cloned.1.call-update
  11.2 0.0 reduce-scatter.8.cloned.1.call-start
  11.2 54.0 %reduce-scatter.6.cloned.1.call-done = f32[1024,128]{1,0:T(8,128)} async-done(((f32[8192,128]{1,0:T(8,128)}), f32[1024,128]{1,0:T(8,128)}) %reduce-scatter.6.cloned.1.call-update) | async-done | bytes 524304 | tf_op jit(solution)/shard_map/reduce_scatter | solution.py:16
  65.3 0.0 copy-done
  65.3 4.1 %fusion.6 = f32[1024,128]{1,0:T(8,128)} fusion(bf16[1024,1024]{1,0:T(8,128)(2,1)S(1)} %copy-done, f32[1024,128]{1,0:T(8,128)} %reduce-scatter.6.cloned.1.call-done), kind=kOutput, calls=%fused_computation.12 | convolution fusion | flops 1610612736 | bytes 3145728 | tf_op jit(solution)/shard_map/dot_general | solution.py:20
  69.4 0.0 reduce-scatter.8.cloned.1.call-update
  69.5 0.0 reduce-scatter.4.cloned.1.call-start
  69.5 5.9 %fusion.5 = f32[1024,1024]{1,0:T(8,128)} fusion(bf16[1024,1024]{1,0:T(8,128)(2,1)S(1)} %copy-done, bf16[1024,1024]{1,0:T(8,128)(2,1)} %param.7), kind=kOutput, calls=%fused_computation.11 | convolution fusion | flops 2147483648 | bytes 8388608 | tf_op jit(solution)/shard_map/dot_general | solution.py:28
  75.4 0.0 copy-start.2
  75.4 0.0 copy-start.4
  75.4 0.0 copy-start.5
  75.4 0.0 reduce-scatter.4.cloned.1.call-update
  75.5 0.0 all-reduce.2.cloned.1.call-start
  75.5 1.0 copy-done.2
  76.5 1.0 copy.9
  77.5 0.0 copy-done.4
  77.5 9.8 %all_gather.9 = f32[1024,128]{1,0:T(8,128)S(1)} all-gather(f32[128,128]{1,0:T(8,128)S(1)} %copy-done.4), channel_id=1, replica_groups=mesh['outer'=4,'dev'=8] {'dev'}, dimensions={0}, use_global_device_ids=true | all-gather | bytes 589824 | tf_op jit(solution)/shard_map/all_gather | solution.py:33
  87.2 16.5 %reduce-scatter.8.cloned.1.call-done = f32[128,128]{1,0:T(8,128)} async-done(((f32[1024,128]{1,0:T(8,128)}), f32[128,128]{1,0:T(8,128)}) %reduce-scatter.8.cloned.1.call-update) | async-done | bytes 65552 | tf_op jit(solution)/shard_map/reduce_scatter | solution.py:19
  103.7 0.0 all-reduce.2.cloned.1.call-update
  103.7 0.0 copy-done.5
  103.8 9.8 %all_gather.10 = f32[1024,128]{1,0:T(8,128)S(1)} all-gather(f32[128,128]{1,0:T(8,128)S(1)} %copy-done.5), channel_id=1, replica_groups=mesh['outer'=4,'dev'=8] {'dev'}, dimensions={0}, use_global_device_ids=true | all-gather | bytes 589824 | tf_op jit(solution)/shard_map/all_gather | solution.py:34
  113.5 44.7 %reduce-scatter.4.cloned.1.call-done = f32[128,1024]{1,0:T(8,128)} async-done(((f32[1024,1024]{1,0:T(8,128)}), f32[128,1024]{1,0:T(8,128)}) %reduce-scatter.4.cloned.1.call-update) | async-done | bytes 524304 | tf_op jit(solution)/shard_map/reduce_scatter | solution.py:27
  158.3 36.5 %all-reduce.2.cloned.1.call-done = f32[128,128]{1,0:T(8,128)} async-done(((f32[128,128]{1,0:T(8,128)}), f32[128,128]{1,0:T(8,128)}) %all-reduce.2.cloned.1.call-update) | async-done | bytes 65552 | tf_op jit(solution)/shard_map/psum | solution.py:25
  194.8 0.0 copy-start.1
  194.8 1.7 fusion.3
  196.5 0.0 copy-start.3
  196.5 2.4 %divide_convert_fusion = (bf16[128,128]{1,0:T(8,128)(2,1)S(1)}, f32[128,128]{1,0:T(8,128)}) fusion(f32[128,128]{1,0:T(8,128)S(1)} %fusion.3, f32[128,128]{1,0:T(8,128)} %all-reduce.2.cloned.1.call-done, f32[1024,128]{1,0:T(8,128)S(1)} %all_gather.10, f32[128,1024]{1,0:T(8,128)} %reduce-scatter.4.cloned.1.call-done), kind=kOutput, calls=%fused_computation.10 | convolution fusion | flops 201605120 | bytes 1277952 | tf_op jit(solution)/shard_map/dot_general | solution.py:36
  198.9 9.2 %all_gather.11 = bf16[1024,128]{1,0:T(8,128)(2,1)S(1)} all-gather(bf16[128,128]{1,0:T(8,128)(2,1)S(1)} %get-tuple-element.6), channel_id=1, replica_groups=mesh['outer'=4,'dev'=8] {'dev'}, dimensions={0}, use_global_device_ids=true | all-gather | bytes 294912 | tf_op jit(solution)/shard_map/all_gather | solution.py:45
  208.1 0.0 copy-done.1
  208.1 0.8 fusion.1
  209.0 0.0 copy-done.3
  209.0 1.0 copy.10
Async XLA Ops:
  7.2 58.1 %copy-start = (bf16[1024,1024]{1,0:T(8,128)(2,1)S(1)}, bf16[1024,1024]{1,0:T(8,128)(2,1)}, u32[]{:S(2)}) copy-start(bf16[1024,1024]{1,0:T(8,128)(2,1)} %param.8) | copy-start | bytes 6291460
  7.2 58.1 %reduce-scatter.6.cloned.1.call-start = ((), (), s32[]{:S(2)}) async-start(), calls=%async_computation.4 | async-start | bytes 4718592 | tf_op jit(solution)/shard_map/reduce_scatter | solution.py:16
  11.2 92.5 %reduce-scatter.8.cloned.1.call-start = ((), (), s32[]{:S(2)}) async-start(), calls=%async_computation.5 | async-start | bytes 589824 | tf_op jit(solution)/shard_map/reduce_scatter | solution.py:19
  69.5 88.8 %reduce-scatter.4.cloned.1.call-start = ((), (), s32[]{:S(2)}) async-start(), calls=%async_computation.3 | async-start | bytes 4718592 | tf_op jit(solution)/shard_map/reduce_scatter | solution.py:27
  75.4 1.0 copy-start.2
  75.4 2.0 copy-start.4
  75.4 28.3 %copy-start.5 = (f32[128,128]{1,0:T(8,128)S(1)}, f32[128,128]{1,0:T(8,128)}, u32[]{:S(2)}) copy-start(f32[128,128]{1,0:T(8,128)} %param.11) | copy-start | bytes 196612
  75.5 119.3 %all-reduce.2.cloned.1.call-start = ((), (), s32[]{:S(2)}) async-start(), calls=%async_computation.6 | async-start | bytes 131072 | tf_op jit(solution)/shard_map/psum | solution.py:25
  194.8 13.4 %copy-start.1 = (f32[1024,128]{0,1:T(8,128)S(1)}, f32[1024,128]{0,1:T(8,128)}, u32[]{:S(2)}) copy-start(f32[1024,128]{0,1:T(8,128)} %copy.9) | copy-start | bytes 1572868
  196.5 12.5 %copy-start.3 = (f32[128,128]{1,0:T(8,128)}, f32[128,128]{1,0:T(8,128)S(1)}, u32[]{:S(2)}) copy-start(f32[128,128]{1,0:T(8,128)S(1)} %fusion.3) | copy-start | bytes 196612
Sparse Core Ops, SparseCore 0:
  11.3 53.8 reduce-scatter.5
  69.6 34.0 reduce-scatter.7
  107.1 51.1 reduce-scatter.3
  160.5 34.2 all-reduce.1
where the time goes:
time: 217 us
  waiting for transfers between devices  152 us (70%)
  blocking collectives  28.8 us (13%)
  matrix products  15 us (7%)
  between operations  13.8 us (6%)
  other arithmetic  3.94 us (2%)
  local copies, waits for them, and re-layouts  2.99 us (1%)
    reduce_scatter x1, waiting for transfers between devices, on_device(): lax.psum_scatter(local_grad, 'dev', scatter_dimension=0, tiled=True)  54 us
    reduce_scatter x1, waiting for transfers between devices, on_device(): lax.psum_scatter(jnp.dot(columns.T, p_old, preferred_element_type=jnp.flo...  44.7 us
    psum x1, waiting for transfers between devices, on_device(): projected = lax.psum(projected, 'outer')  36.5 us
    reduce_scatter x1, waiting for transfers between devices, on_device(): lax.psum_scatter(jnp.dot(columns.T, grad_rows, precision=lax.Precision.HI...  16.5 us
    all_gather x1, blocking collectives, on_device(): second_piece = lax.all_gather(v_old, 'dev', axis=0, tiled=True)  9.79 us
    all_gather x1, blocking collectives, on_device(): first_piece = lax.all_gather(m_old, 'dev', axis=0, tiled=True)  9.77 us
    all_gather x1, blocking collectives, on_device(): lax.all_gather(direction, 'dev', axis=0, tiled=True)  9.25 us
    dot_general x1, matrix products, on_device(): jnp.dot(columns.T, p_old, preferred_element_type=jnp.float32)  5.92 us
  transfers between devices with their start and end apart: 4, of which 4 were waited for; matrix products, arithmetic and copies ran while one was open for 3% of the time, Pallas kernels for 0%

commit v1 on v0

--- a/solution.py
+++ b/solution.py
@@ -30,8 +30,11 @@
         scatter_dimension=0,
         tiled=True,
     )
-    first_piece = lax.all_gather(m_old, "dev", axis=0, tiled=True)
-    second_piece = lax.all_gather(v_old, "dev", axis=0, tiled=True)
+    first_piece, second_piece = jnp.split(
+        lax.all_gather(jnp.concatenate([m_old, v_old], axis=1), "dev", axis=0, tiled=True),
+        [m_old.shape[1]],
+        axis=1,
+    )
     first = jnp.dot(margin_rows, first_piece, precision=lax.Precision.HIGHEST)
     second = jnp.dot(margin_rows * margin_rows, second_piece, precision=lax.Precision.HIGHEST)
     m_new = beta_mean * first + (1.0 - beta_mean) * projected

time: 217 us -> 242 us (1.12)
  waiting for transfers between devices: 152 us -> 198 us
  blocking collectives: 28.8 us -> 9.25 us
    all_gather x0 -> x1, waiting for transfers between devices: none -> 25.1 us  [on_device(): lax.all_gather(jnp.concatenate([m_old, v_old], axis=1), 'dev', axis=0, ti...]
    all_gather x2 -> x0, blocking collectives: 19.6 us -> none  [the longest x1 9.79 us: on_device(): second_piece = lax.all_gather(v_old, 'dev', axis=0, tiled=True)]
    reduce_scatter x1, waiting for transfers between devices: 16.5 us -> 27.5 us  [on_device(): lax.psum_scatter(jnp.dot(columns.T, grad_rows, precision=lax.Precision.HI...]
    reduce_scatter x1, waiting for transfers between devices: 44.7 us -> 54.4 us  [on_device(): lax.psum_scatter(jnp.dot(columns.T, p_old, preferred_element_type=jnp.flo...]
  transfers between devices with their start and end apart: 4 -> 5, of which waited for: 4 -> 5; matrix products, arithmetic and copies ran while one was open for 3% -> 3% of each run, Pallas kernels for 0% -> 0%
where the time goes in v1:
time: 242 us
  waiting for transfers between devices  198 us (82%)
  matrix products  15.3 us (6%)
  between operations  13.9 us (6%)
  blocking collectives  9.25 us (4%)
  other arithmetic  4.61 us (2%)
    reduce_scatter x1, waiting for transfers between devices, on_device(): lax.psum_scatter(jnp.dot(columns.T, p_old, preferred_element_type=jnp.flo...  54.4 us
    reduce_scatter x1, waiting for transfers between devices, on_device(): lax.psum_scatter(local_grad, 'dev', scatter_dimension=0, tiled=True)  54 us
    psum x1, waiting for transfers between devices, on_device(): projected = lax.psum(projected, 'outer')  36.5 us
    reduce_scatter x1, waiting for transfers between devices, on_device(): lax.psum_scatter(jnp.dot(columns.T, grad_rows, precision=lax.Precision.HI...  27.5 us
    all_gather x1, waiting for transfers between devices, on_device(): lax.all_gather(jnp.concatenate([m_old, v_old], axis=1), 'dev', axis=0, ti...  25.1 us
    all_gather x1, blocking collectives, on_device(): lax.all_gather(direction, 'dev', axis=0, tiled=True)  9.25 us
    dot_general x1, matrix products, on_device(): jnp.dot(columns.T, p_old, preferred_element_type=jnp.float32)  5.92 us
  transfers between devices with their start and end apart: 5, of which 5 were waited for; matrix products, arithmetic and copies ran while one was open for 3% of the time, Pallas kernels for 0%

profile of v1, /device:TPU:0, one launch (start us, length us, event | category | flops | bytes accessed | tf_op | source)
XLA Modules:
  0.0 241.9 jit_solution(13134546343763400778)
XLA Ops:
  7.2 0.0 copy-start
  7.2 0.0 reduce-scatter.6.cloned.1.call-start
  7.2 3.9 %bitcast_convert_fusion = f32[8192,128]{1,0:T(8,128)} fusion(bf16[1,8192,128]{2,1,0:T(8,128)(2,1)} %param.6), kind=kLoop, calls=%fused_computation | loop fusion | flops 1048576 | bytes 6291456 | tf_op jit(solution)/shard_map/convert_element_type | solution.py:15
  11.2 0.0 reduce-scatter.6.cloned.1.call-update
  11.2 0.0 copy-start.3
  11.2 0.0 copy-start.4
  11.2 0.0 reduce-scatter.8.cloned.1.call-start
  11.3 54.0 %reduce-scatter.6.cloned.1.call-done = f32[1024,128]{1,0:T(8,128)} async-done(((f32[8192,128]{1,0:T(8,128)}), f32[1024,128]{1,0:T(8,128)}) %reduce-scatter.6.cloned.1.call-update) | async-done | bytes 524304 | tf_op jit(solution)/shard_map/reduce_scatter | solution.py:16
  65.3 0.0 copy-done
  65.3 4.1 %fusion.8 = f32[1024,128]{1,0:T(8,128)} fusion(bf16[1024,1024]{1,0:T(8,128)(2,1)S(1)} %copy-done, f32[1024,128]{1,0:T(8,128)} %reduce-scatter.6.cloned.1.call-done), kind=kOutput, calls=%fused_computation.15 | convolution fusion | flops 1610612736 | bytes 3145728 | tf_op jit(solution)/shard_map/dot_general | solution.py:20
  69.4 0.0 reduce-scatter.8.cloned.1.call-update
  69.5 0.0 all-gather.2.cloned.1.call-start
  69.5 0.0 copy-done.3
  69.5 0.0 copy-done.4
  69.5 0.7 pad_maximum_fusion
  70.2 0.0 all-gather.2.cloned.1.call-update
  70.2 0.0 reduce-scatter.4.cloned.1.call-start
  70.3 5.9 %fusion.7 = f32[1024,1024]{1,0:T(8,128)} fusion(bf16[1024,1024]{1,0:T(8,128)(2,1)S(1)} %copy-done, bf16[1024,1024]{1,0:T(8,128)(2,1)} %param.7), kind=kOutput, calls=%fused_computation.14 | convolution fusion | flops 2147483648 | bytes 8388608 | tf_op jit(solution)/shard_map/dot_general | solution.py:28
  76.2 0.0 copy-start.1
  76.2 0.0 reduce-scatter.4.cloned.1.call-update
  76.2 0.0 all-reduce.2.cloned.1.call-start
  76.3 27.5 %reduce-scatter.8.cloned.1.call-done = f32[128,128]{1,0:T(8,128)} async-done(((f32[1024,128]{1,0:T(8,128)}), f32[128,128]{1,0:T(8,128)}) %reduce-scatter.8.cloned.1.call-update) | async-done | bytes 65552 | tf_op jit(solution)/shard_map/reduce_scatter | solution.py:19
  103.7 0.0 all-reduce.2.cloned.1.call-update
  103.7 0.0 copy-done.1
  103.8 0.2 copy.9
  104.0 25.1 %all-gather.2.cloned.1.call-done = f32[1024,256]{1,0:T(8,128)} async-done(((f32[128,256]{1,0:T(8,128)}), f32[1024,256]{1,0:T(8,128)}) %all-gather.2.cloned.1.call-update) | async-done | bytes 1048592 | tf_op jit(solution)/shard_map/all_gather | solution.py:34
  129.0 54.4 %reduce-scatter.4.cloned.1.call-done = f32[128,1024]{1,0:T(8,128)} async-done(((f32[1024,1024]{1,0:T(8,128)}), f32[128,1024]{1,0:T(8,128)}) %reduce-scatter.4.cloned.1.call-update) | async-done | bytes 524304 | tf_op jit(solution)/shard_map/reduce_scatter | solution.py:27
  183.4 36.5 %all-reduce.2.cloned.1.call-done = f32[128,128]{1,0:T(8,128)} async-done(((f32[128,128]{1,0:T(8,128)}), f32[128,128]{1,0:T(8,128)}) %all-reduce.2.cloned.1.call-update) | async-done | bytes 65552 | tf_op jit(solution)/shard_map/psum | solution.py:25
  219.9 1.8 fusion.3
  221.8 0.0 copy-start.2
  221.8 2.5 %divide_convert_fusion = (bf16[128,128]{1,0:T(8,128)(2,1)S(1)}, f32[128,128]{1,0:T(8,128)}) fusion(f32[128,128]{1,0:T(8,128)S(1)} %fusion.3, f32[128,128]{1,0:T(8,128)} %all-reduce.2.cloned.1.call-done, f32[1024,256]{1,0:T(8,128)} %all-gather.2.cloned.1.call-done, f32[128,1024]{1,0:T(8,128)} %reduce-scatter.4.cloned.1.call-done), kind=kOutput, calls=%fused_computation.13 | convolution fusion | flops 201605120 | bytes 1277952 | tf_op jit(solution)/shard_map/dot_general | solution.py:39
  224.3 9.2 %all_gather.7 = bf16[1024,128]{1,0:T(8,128)(2,1)S(1)} all-gather(bf16[128,128]{1,0:T(8,128)(2,1)S(1)} %get-tuple-element.6), channel_id=1, replica_groups=mesh['outer'=4,'dev'=8] {'dev'}, dimensions={0}, use_global_device_ids=true | all-gather | bytes 294912 | tf_op jit(solution)/shard_map/all_gather | solution.py:48
  233.5 0.8 fusion.1
  234.4 0.0 copy-done.2
  234.4 1.0 copy.10
Async XLA Ops:
  7.2 58.1 %copy-start = (bf16[1024,1024]{1,0:T(8,128)(2,1)S(1)}, bf16[1024,1024]{1,0:T(8,128)(2,1)}, u32[]{:S(2)}) copy-start(bf16[1024,1024]{1,0:T(8,128)(2,1)} %param.8) | copy-start | bytes 6291460
  7.2 58.1 %reduce-scatter.6.cloned.1.call-start = ((), (), s32[]{:S(2)}) async-start(), calls=%async_computation.5 | async-start | bytes 4718592 | tf_op jit(solution)/shard_map/reduce_scatter | solution.py:16
  11.2 58.3 %copy-start.3 = (f32[128,128]{1,0:T(8,128)S(1)}, f32[128,128]{1,0:T(8,128)}, u32[]{:S(2)}) copy-start(f32[128,128]{1,0:T(8,128)} %param.11) | copy-start | bytes 196612
  11.2 58.3 %copy-start.4 = (f32[128,128]{1,0:T(8,128)S(1)}, f32[128,128]{1,0:T(8,128)}, u32[]{:S(2)}) copy-start(f32[128,128]{1,0:T(8,128)} %param.10) | copy-start | bytes 196612
  11.2 92.5 %reduce-scatter.8.cloned.1.call-start = ((), (), s32[]{:S(2)}) async-start(), calls=%async_computation.6 | async-start | bytes 589824 | tf_op jit(solution)/shard_map/reduce_scatter | solution.py:19
  69.5 59.6 %all-gather.2.cloned.1.call-start = ((), (), s32[]{:S(2)}) async-start(), calls=%async_computation.4 | async-start | bytes 1179648 | tf_op jit(solution)/shard_map/all_gather | solution.py:34
  70.2 113.2 %reduce-scatter.4.cloned.1.call-start = ((), (), s32[]{:S(2)}) async-start(), calls=%async_computation.3 | async-start | bytes 4718592 | tf_op jit(solution)/shard_map/reduce_scatter | solution.py:27
  76.2 27.6 %copy-start.1 = (f32[1024,128]{1,0:T(8,128)S(1)}, f32[1024,128]{1,0:T(8,128)}, u32[]{:S(2)}) copy-start(f32[1024,128]{1,0:T(8,128)} %param.9) | copy-start | bytes 1572868
  76.2 143.7 %all-reduce.2.cloned.1.call-start = ((), (), s32[]{:S(2)}) async-start(), calls=%async_computation.7 | async-start | bytes 131072 | tf_op jit(solution)/shard_map/psum | solution.py:25
  221.8 12.6 %copy-start.2 = (f32[128,128]{1,0:T(8,128)}, f32[128,128]{1,0:T(8,128)S(1)}, u32[]{:S(2)}) copy-start(f32[128,128]{1,0:T(8,128)S(1)} %fusion.3) | copy-start | bytes 196612
Sparse Core Ops, SparseCore 0:
  11.3 53.8 reduce-scatter.5
  69.6 34.0 reduce-scatter.7
  105.6 23.3 all-gather.1
  132.2 51.1 reduce-scatter.3
  185.6 34.2 all-reduce.1
